TPU v7x, 128 devices: a whole 4x4x4 slice. The times are simulated.
128 devices in a mesh: row: 16 (over z, x), col: 8 (over y, core).
Axes of the slice: x: 4, y: 4, z: 4, core: 2. Of those that a mesh axis runs over, the one named last changes fastest.
Arguments:
- tokens: bfloat16 [2048, 4096], P('row', 'col'), may hold values from -6 to 6
- up_weight: bfloat16 [128, 8, 128, 128], P(('col', 'row')), may hold values from -0.1875 to 0.1875
- up_rows: int32 [128, 8], P('col'), may hold values from 0 to 31, as said below
- down_weight: bfloat16 [128, 8, 128, 128], P(('col', 'row')), may hold values from -0.09375 to 0.09375
- down_cols: int32 [128, 8], P('col'), may hold values from 0 to 31, as said below
- grad_out: bfloat16 [2048, 4096], P('row', 'col'), may hold values from -6 to 6
Outputs:
- layer_out: bfloat16 [2048, 4096], P('row', 'col')
- grad_tokens: bfloat16 [2048, 4096], P('row', 'col')
- grad_up: bfloat16 [128, 8, 128, 128], P(('col', 'row'))
- grad_down: bfloat16 [128, 8, 128, 128], P(('col', 'row'))
Inputs may be any that keep to these rules, and one draw needn't show every extreme that they name: `up_rows`: row j lists 8 distinct block rows of the up projection's block column j in rising order; they are that block column's only nonzero blocks. `down_cols`: row i lists 8 distinct block columns of the down projection's block row i in rising order; they are that block row's only nonzero blocks.
All inputs are finite; a program needn't handle non-finite values.
Results may differ from a plain program's by a relative error of at most 0.019.
Values may be sent and summed in bfloat16 or wider, within the bound.
No kernel may reach another device: no remote copies, remote signals or barrier semaphores. Data moves between devices by JAX's collectives and lax.ppermute only.
A program may use at most 128 MiB of HBM per device.

v0:
```python
import math
import jax
import jax.numpy as jnp
from jax import lax
from jax.sharding import PartitionSpec as P


def gelu_tanh(values):
    return jax.nn.gelu(values, approximate=True)


def up_apply(token_blocks, panel_blocks, row_ids):
    summed = jnp.zeros(
        (token_blocks.shape[0], panel_blocks.shape[0], panel_blocks.shape[3]), jnp.float32
    )
    for slot_index in range(panel_blocks.shape[1]):
        picked = jnp.take(token_blocks, row_ids[:, slot_index], axis=1)
        summed = summed + jnp.einsum(
            "tja,jab->tjb", picked, panel_blocks[:, slot_index], preferred_element_type=jnp.float32
        )
    return summed


def up_transpose(grad_piece, panel_blocks, row_ids, block_count):
    summed = jnp.zeros((grad_piece.shape[0], block_count, panel_blocks.shape[2]), jnp.float32)
    for slot_index in range(panel_blocks.shape[1]):
        product = jnp.einsum(
            "tjb,jab->tja",
            grad_piece,
            panel_blocks[:, slot_index],
            preferred_element_type=jnp.float32,
        )
        summed = summed.at[:, row_ids[:, slot_index], :].add(product)
    return summed


def down_apply(hidden_piece, grad_blocks, panel_blocks, col_ids, block_count):
    tok_rows = hidden_piece.shape[0]
    out_part = jnp.zeros((tok_rows, block_count, panel_blocks.shape[3]), jnp.float32)
    grad_piece = jnp.zeros((tok_rows, panel_blocks.shape[0], panel_blocks.shape[2]), jnp.float32)
    for slot_index in range(panel_blocks.shape[1]):
        weight_slot = panel_blocks[:, slot_index]
        product = jnp.einsum(
            "tia,iab->tib", hidden_piece, weight_slot, preferred_element_type=jnp.float32
        )
        out_part = out_part.at[:, col_ids[:, slot_index], :].add(product)
        picked = jnp.take(grad_blocks, col_ids[:, slot_index], axis=1)
        grad_piece = grad_piece + jnp.einsum(
            "tib,iab->tia", picked, weight_slot, preferred_element_type=jnp.float32
        )
    return (out_part, grad_piece)


def per_device(tokens, up_weight, up_rows, down_weight, down_cols, grad_out):
    tok_rows = tokens.shape[0]
    block_size = up_weight.shape[2]
    slot_count = up_weight.shape[1]
    token_whole, grad_whole = (
        lax.all_gather(tokens, "col", axis=1, tiled=True),
        lax.all_gather(grad_out, "col", axis=1, tiled=True),
    )
    block_count = token_whole.shape[1] // block_size
    token_blocks = token_whole.reshape(tok_rows, block_count, block_size)
    grad_blocks = grad_whole.reshape(tok_rows, block_count, block_size)
    row_ids = up_rows
    pre_act = up_apply(token_blocks, lax.all_gather(up_weight, "row", axis=0, tiled=True), row_ids)
    hidden = gelu_tanh(pre_act).astype(jnp.bfloat16)
    hidden_piece = hidden
    col_ids = down_cols
    added, grad_piece = down_apply(
        hidden_piece,
        grad_blocks,
        lax.all_gather(down_weight, "row", axis=0, tiled=True),
        col_ids,
        block_count,
    )
    grad_hidden = grad_piece
    out_sum = lax.psum_scatter(
        added.astype(jnp.bfloat16), "col", scatter_dimension=1, tiled=True
    ).astype(jnp.float32)
    layer_out = out_sum.reshape(tok_rows, -1).astype(jnp.bfloat16)
    pull_back = jax.vjp(gelu_tanh, pre_act)[1]
    grad_pre = pull_back(grad_hidden)[0].astype(jnp.bfloat16)
    row_ids = up_rows
    grad_piece = grad_pre
    input_part = up_transpose(
        grad_piece, lax.all_gather(up_weight, "row", axis=0, tiled=True), row_ids, block_count
    )
    input_sum = lax.psum_scatter(
        input_part.astype(jnp.bfloat16), "col", scatter_dimension=1, tiled=True
    ).astype(jnp.float32)
    grad_tokens = input_sum.reshape(tok_rows, -1).astype(jnp.bfloat16)
    hidden_piece = hidden
    col_ids = down_cols
    terms_list = []
    for down_slot_index in range(slot_count):
        down_picked = jnp.take(grad_blocks, col_ids[:, down_slot_index], axis=1)
        terms_list.append(
            jnp.einsum(
                "tia,tib->iab", hidden_piece, down_picked, preferred_element_type=jnp.float32
            )
        )
    down_sum = lax.psum_scatter(
        jnp.stack(terms_list, axis=1).astype(jnp.bfloat16), "row", scatter_dimension=0, tiled=True
    ).astype(jnp.float32)
    grad_piece = grad_pre
    row_ids = up_rows
    terms_list = []
    for slot_index in range(slot_count):
        picked = jnp.take(token_blocks, row_ids[:, slot_index], axis=1)
        terms_list.append(
            jnp.einsum("tja,tjb->jab", picked, grad_piece, preferred_element_type=jnp.float32)
        )
    up_sum = lax.psum_scatter(
        jnp.stack(terms_list, axis=1).astype(jnp.bfloat16), "row", scatter_dimension=0, tiled=True
    ).astype(jnp.float32)
    grad_scale = 1.0 / math.sqrt(tok_rows * lax.axis_size("row"))
    grad_up = (up_sum * grad_scale).astype(jnp.bfloat16)
    grad_down = (down_sum * grad_scale).astype(jnp.bfloat16)
    return (layer_out, grad_tokens, grad_up, grad_down)


def solution(mesh):
    return jax.shard_map(
        per_device,
        mesh=mesh,
        in_specs=(
            P("row", "col"),
            P(("col", "row"), None, None, None),
            P("col", None),
            P(("col", "row"), None, None, None),
            P("col", None),
            P("row", "col"),
        ),
        out_specs=(
            P("row", "col"),
            P("row", "col"),
            P(("col", "row"), None, None, None),
            P(("col", "row"), None, None, None),
        ),
        check_vma=False,
    )
```

profile of v0, /device:TPU:1, one launch (start us, length us, event | category | flops | bytes accessed | tf_op | source)
XLA Modules:
  0.0 460.6 jit_solution(11785073834474695060)
XLA Ops:
  8.9 1.7 copy.108
  16.1 21.2 %all-gather.5.cloned.1.call-done = bf16[128,4096]{0,1:T(8,128)(2,1)} async-done(((bf16[128,512]{0,1:T(8,128)(2,1)}), bf16[128,4096]{0,1:T(8,128)(2,1)}) %all-gather.5.cloned.1.call-update) | async-done | bytes 1048592 | tf_op jit(solution)/shard_map/all_gather | solution.py:59
  48.1 14.8 %all-gather.11.cloned.1.call-done = bf16[128,4096]{0,1:T(8,128)(2,1)} async-done(((bf16[128,512]{0,1:T(8,128)(2,1)}), bf16[128,4096]{0,1:T(8,128)(2,1)}) %all-gather.11.cloned.1.call-update) | async-done | bytes 1048592 | tf_op jit(solution)/shard_map/all_gather | solution.py:60
  75.1 41.1 %all-gather.7.cloned.1.call-done = bf16[16,8,128,128]{3,2,0,1:T(8,128)(2,1)} async-done(((bf16[1,8,128,128]{3,2,0,1:T(8,128)(2,1)}), bf16[16,8,128,128]{3,2,0,1:T(8,128)(2,1)}) %all-gather.7.cloned.1.call-update) | async-done | bytes 4194320 | tf_op jit(solution)/shard_map/all_gather | solution.py:66
  122.9 46.6 %all-gather.9.cloned.1.call-done = bf16[16,8,128,128]{3,2,0,1:T(8,128)(2,1)} async-done(((bf16[1,8,128,128]{3,2,0,1:T(8,128)(2,1)}), bf16[16,8,128,128]{3,2,0,1:T(8,128)(2,1)}) %all-gather.9.cloned.1.call-update) | async-done | bytes 4194320 | tf_op jit(solution)/shard_map/all_gather | solution.py:73
  169.5 2.3 fusion.83
  172.0 2.6 scatter_fusion
  174.6 2.3 fusion.84
  176.9 2.6 scatter_fusion.1
  179.5 2.3 fusion.85
  181.8 2.6 scatter_fusion.2
  184.5 2.3 fusion.86
  186.8 2.6 scatter_fusion.3
  189.4 2.3 fusion.87
  191.7 2.6 scatter_fusion.4
  194.3 2.3 fusion.88
  196.6 2.6 scatter_fusion.5
  199.2 2.3 fusion.89
  201.5 2.8 scatter_fusion.6
  204.3 2.3 fusion.90
  206.6 2.6 scatter_fusion.7
  210.4 1.7 fusion.56
  212.1 1.8 convolution_add_fusion.6
  217.7 2.5 fusion.75
  220.4 2.6 scatter_fusion.8
  223.0 2.5 fusion.76
  225.5 2.6 scatter_fusion.9
  228.1 2.5 fusion.77
  230.6 2.6 scatter_fusion.10
  233.2 2.5 fusion.78
  235.7 2.6 scatter_fusion.11
  238.3 2.5 fusion.79
  240.8 2.6 scatter_fusion.12
  243.4 2.5 fusion.80
  245.9 2.6 scatter_fusion.13
  248.6 2.5 fusion.81
  251.0 2.6 scatter_fusion.14
  253.6 2.5 fusion.82
  256.1 2.8 scatter_fusion.15
  260.1 2.4 fusion.3
  262.5 2.3 fusion.19
  264.8 2.3 fusion.5
  273.4 2.4 fusion.17
  275.8 2.3 fusion.21
  288.2 13.9 %reduce-scatter.11.cloned.1.call-done = bf16[128,4,128]{2,0,1:T(8,128)(2,1)} async-done(((bf16[128,32,128]{2,0,1:T(8,128)(2,1)}), bf16[128,4,128]{2,0,1:T(8,128)(2,1)}) %reduce-scatter.11.cloned.1.call-update) | async-done | bytes 131088 | tf_op jit(solution)/shard_map/reduce_scatter | solution.py:89
  303.9 145.3 %all-reduce.5.cloned.1.call-done = (bf16[16,8,128,128]{3,2,0,1:T(8,128)(2,1)}, bf16[16,8,128,128]{3,2,0,1:T(8,128)(2,1)}) async-done(((bf16[16,8,128,128]{3,2,0,1:T(8,128)(2,1)}, bf16[16,8,128,128]{3,2,0,1:T(8,128)(2,1)}), (bf16[16,8,128,128]{3,2,0,1:T(8,128)(2,1)}, bf16[16,8,128,128]{3,2,0,1:T(8,128)(2,1)})) %all-reduce.5.cloned.1.call-update) | async-done | bytes 8388624
  449.2 2.3 fusion.91
  451.5 2.3 fusion.92
  (138 shorter events, 61.2 us)
Async XLA Ops:
  7.2 30.2 %all-gather.5.cloned.1.call-start = ((), (), s32[]{:S(2)}) async-start(), calls=%async_computation.2 | async-start | bytes 1179648 | tf_op jit(solution)/shard_map/all_gather | solution.py:59
  8.9 54.0 %all-gather.11.cloned.1.call-start = ((), (), s32[]{:S(2)}) async-start(), calls=%async_computation.6 | async-start | bytes 1179648 | tf_op jit(solution)/shard_map/all_gather | solution.py:60
  10.6 105.5 %all-gather.7.cloned.1.call-start = ((), (), s32[]{:S(2)}) async-start(), calls=%async_computation.3 | async-start | bytes 4456448 | tf_op jit(solution)/shard_map/all_gather | solution.py:66
  11.4 158.1 %all-gather.9.cloned.1.call-start = ((), (), s32[]{:S(2)}) async-start(), calls=%async_computation.4 | async-start | bytes 4456448 | tf_op jit(solution)/shard_map/all_gather | solution.py:73
  12.0 274.5 %reduce-scatter.9.cloned.1.call-start = ((), (), s32[]{:S(2)}) async-start(), calls=%async_computation.5 | async-start | bytes 1179648 | tf_op jit(solution)/shard_map/reduce_scatter | solution.py:78
  39.6 76.6 %copy-start.2 = (bf16[16,128,128]{2,1,0:T(8,128)(2,1)}, bf16[16,128,128]{2,1,0:T(8,128)(2,1)S(1)}, u32[]{:S(2)}) copy-start(bf16[16,128,128]{2,1,0:T(8,128)(2,1)S(1)} %gather_fusion) | copy-start | bytes 1572868
  46.0 74.5 %copy-start.16 = (bf16[16,128,128]{2,1,0:T(8,128)(2,1)}, bf16[16,128,128]{2,1,0:T(8,128)(2,1)S(1)}, u32[]{:S(2)}) copy-start(bf16[16,128,128]{2,1,0:T(8,128)(2,1)S(1)} %gather_fusion.5) | copy-start | bytes 1572868
  46.6 74.2 %copy-start.14 = (bf16[16,128,128]{2,1,0:T(8,128)(2,1)}, bf16[16,128,128]{2,1,0:T(8,128)(2,1)S(1)}, u32[]{:S(2)}) copy-start(bf16[16,128,128]{2,1,0:T(8,128)(2,1)S(1)} %gather_fusion.6) | copy-start | bytes 1572868
  65.2 145.2 %copy-start.3 = (bf16[16,128,128]{2,1,0:T(8,128)(2,1)}, bf16[16,128,128]{2,1,0:T(8,128)(2,1)S(1)}, u32[]{:S(2)}) copy-start(bf16[16,128,128]{2,1,0:T(8,128)(2,1)S(1)} %gather_fusion.8) | copy-start | bytes 1572868
  75.1 44.3 %copy-start.22 = (bf16[16,128,128]{2,1,0:T(8,128)(2,1)S(1)}, bf16[16,128,128]{2,1,0:T(8,128)(2,1)}, u32[]{:S(2)}) copy-start(bf16[16,128,128]{2,1,0:T(8,128)(2,1)} %gather_fusion.2) | copy-start | bytes 1572868
  116.2 3.2 copy-start
  116.2 3.6 copy-start.20
  117.7 2.4 copy-start.18
  120.1 1.1 copy-start.26
  210.3 3.6 copy-start.12
  210.3 91.8 %reduce-scatter.11.cloned.1.call-start = ((), (), s32[]{:S(2)}) async-start(), calls=%async_computation.7 | async-start | bytes 1179648 | tf_op jit(solution)/shard_map/reduce_scatter | solution.py:89
  210.4 3.5 copy-start.1
  210.4 4.1 copy-start.10
  212.1 2.9 copy-start.8
  213.9 1.7 copy-start.6
  214.5 1.6 copy-start.4
  215.0 1.6 copy-start.24
  215.1 1.6 copy-start.28
  260.1 8.3 %copy-start.21 = (bf16[16,128,128]{2,1,0:T(8,128)(2,1)S(1)}, bf16[16,128,128]{2,1,0:T(8,128)(2,1)}, u32[]{:S(2)}) copy-start(bf16[16,128,128]{2,1,0:T(8,128)(2,1)} %gather_fusion.3) | copy-start | bytes 1572868
  260.1 7.0 %copy-start.23 = (bf16[16,128,128]{2,1,0:T(8,128)(2,1)S(1)}, bf16[16,128,128]{2,1,0:T(8,128)(2,1)}, u32[]{:S(2)}) copy-start(bf16[16,128,128]{2,1,0:T(8,128)(2,1)} %gather_fusion.2) | copy-start | bytes 1572868
  260.1 9.5 %copy-start.19 = (bf16[16,128,128]{2,1,0:T(8,128)(2,1)S(1)}, bf16[16,128,128]{2,1,0:T(8,128)(2,1)}, u32[]{:S(2)}) copy-start(bf16[16,128,128]{2,1,0:T(8,128)(2,1)} %gather_fusion.4) | copy-start | bytes 1572868
  262.5 8.3 %copy-start.17 = (bf16[16,128,128]{2,1,0:T(8,128)(2,1)S(1)}, bf16[16,128,128]{2,1,0:T(8,128)(2,1)}, u32[]{:S(2)}) copy-start(bf16[16,128,128]{2,1,0:T(8,128)(2,1)} %copy-done.16) | copy-start | bytes 1572868
  264.8 7.3 %copy-start.15 = (bf16[16,128,128]{2,1,0:T(8,128)(2,1)S(1)}, bf16[16,128,128]{2,1,0:T(8,128)(2,1)}, u32[]{:S(2)}) copy-start(bf16[16,128,128]{2,1,0:T(8,128)(2,1)} %copy-done.14) | copy-start | bytes 1572868
  269.6 8.4 %copy-start.13 = (bf16[16,128,128]{2,1,0:T(8,128)(2,1)S(1)}, bf16[16,128,128]{2,1,0:T(8,128)(2,1)}, u32[]{:S(2)}) copy-start(bf16[16,128,128]{2,1,0:T(8,128)(2,1)} %gather_fusion.10) | copy-start | bytes 1572868
  270.9 8.4 %copy-start.11 = (bf16[16,128,128]{2,1,0:T(8,128)(2,1)S(1)}, bf16[16,128,128]{2,1,0:T(8,128)(2,1)}, u32[]{:S(2)}) copy-start(bf16[16,128,128]{2,1,0:T(8,128)(2,1)} %gather_fusion.11) | copy-start | bytes 1572868
  272.1 8.3 %copy-start.9 = (bf16[16,128,128]{2,1,0:T(8,128)(2,1)S(1)}, bf16[16,128,128]{2,1,0:T(8,128)(2,1)}, u32[]{:S(2)}) copy-start(bf16[16,128,128]{2,1,0:T(8,128)(2,1)} %gather_fusion.12) | copy-start | bytes 1572868
  273.3 8.3 %copy-start.7 = (bf16[16,128,128]{2,1,0:T(8,128)(2,1)S(1)}, bf16[16,128,128]{2,1,0:T(8,128)(2,1)}, u32[]{:S(2)}) copy-start(bf16[16,128,128]{2,1,0:T(8,128)(2,1)} %gather_fusion.13) | copy-start | bytes 1572868
  273.4 175.9 %all-reduce.5.cloned.1.call-start = ((), (), s32[]{:S(2)}) async-start(), calls=%async_computation.8 | async-start | bytes 16777216
  275.8 7.1 %copy-start.5 = (bf16[16,128,128]{2,1,0:T(8,128)(2,1)S(1)}, bf16[16,128,128]{2,1,0:T(8,128)(2,1)}, u32[]{:S(2)}) copy-start(bf16[16,128,128]{2,1,0:T(8,128)(2,1)} %gather_fusion.14) | copy-start | bytes 1572868
  278.0 6.0 %copy-start.25 = (bf16[16,128,128]{2,1,0:T(8,128)(2,1)S(1)}, bf16[16,128,128]{2,1,0:T(8,128)(2,1)}, u32[]{:S(2)}) copy-start(bf16[16,128,128]{2,1,0:T(8,128)(2,1)} %gather_fusion.15) | copy-start | bytes 1572868
  285.2 0.7 copy-start.27
Sparse Core Ops, SparseCore 0:
  10.3 26.9 all-gather.4
  39.6 23.2 all-gather.10
  65.0 51.1 all-gather.6
  118.2 51.2 all-gather.8
  210.5 28.6 reduce-scatter.8
  273.5 28.6 reduce-scatter.10
  305.9 143.2 all-reduce.4
where the time goes:
time: 463 us; the launch traced here: 461 us
  waiting for transfers between devices  284 us (61%)
  matrix products  76.9 us (17%)
  other arithmetic  52.9 us (11%)
  local copies, waits for them, and re-layouts  31.5 us (7%)
  between operations  14.8 us (3%)
    unnamed x8, waiting for transfers between devices  147 us
    all_gather x1, waiting for transfers between devices, per_device(): lax.all_gather(down_weight, 'row', axis=0, tiled=True)  46.6 us
    all_gather x1, waiting for transfers between devices, per_device(): lax.all_gather(up_weight, 'row', axis=0, tiled=True)  41.1 us
    all_gather x1, waiting for transfers between devices, per_device(): lax.all_gather(tokens, 'col', axis=1, tiled=True)  21.2 us
    scatter-add x8, other arithmetic, up_transpose(): summed = summed.at[:, row_ids[:, slot_index], :].add(product)  21 us
    scatter-add x8, other arithmetic, down_apply(): out_part = out_part.at[:, col_ids[:, slot_index], :].add(product)  21 us
    dot_general x8, matrix products, up_transpose(): jnp.einsum('tjb,jab->tja', grad_piece, panel_blocks[:, slot_index], prefe...  19.9 us
    dot_general x8, matrix products, down_apply(): jnp.einsum('tia,iab->tib', hidden_piece, weight_slot, preferred_element_t...  18.4 us
  transfers between devices with their start and end apart: 7, of which 6 were waited for; matrix products, arithmetic and copies ran while one was open for 25% of the time, Pallas kernels for 0%

commit v1 on v0

--- a/solution.py
+++ b/solution.py
@@ -56,7 +56,9 @@
     block_size = up_weight.shape[2]
     slot_count = up_weight.shape[1]
     token_whole, grad_whole = (
-        lax.all_gather(tokens, "col", axis=1, tiled=True),
+        jnp.concatenate(
+            lax.all_to_all(jnp.stack([tokens] * lax.axis_size("col")), "col", 0, 0), axis=1
+        ),
         lax.all_gather(grad_out, "col", axis=1, tiled=True),
     )
     block_count = token_whole.shape[1] // block_size

time: 463 us -> 440 us (0.950)
  waiting for transfers between devices: 284 us -> 258 us
  starting transfers between devices: 0.28 us -> 6.17 us
    all_gather x1 -> x0, waiting for transfers between devices: 21.2 us -> none  [per_device(): lax.all_gather(tokens, 'col', axis=1, tiled=True)]
    all_to_all x0 -> x1, waiting for transfers between devices: none -> 18.8 us  [per_device(): lax.all_to_all(jnp.stack([tokens] * lax.axis_size('col')), 'col', 0, 0)]
    all_gather x1, waiting for transfers between devices: 14.8 us -> 0.01 us  [per_device(): lax.all_gather(grad_out, 'col', axis=1, tiled=True)]
    all_gather x1, waiting for transfers between devices: 41.1 us -> 32 us  [per_device(): lax.all_gather(up_weight, 'row', axis=0, tiled=True)]
    all_to_all x0 -> x1, starting transfers between devices: none -> 5.97 us  [per_device(): lax.all_to_all(jnp.stack([tokens] * lax.axis_size('col')), 'col', 0, 0)]
    unnamed x8 -> x7, waiting for transfers between devices: 147 us -> 147 us
  transfers between devices with their start and end apart: 7 -> 7, of which waited for: 6 -> 5; matrix products, arithmetic and copies ran while one was open for 25% -> 25% of each run, Pallas kernels for 0% -> 0%
where the time goes in v1:
time: 440 us; the launch traced here: 438 us
  waiting for transfers between devices  258 us (59%)
  matrix products  76.9 us (17%)
  other arithmetic  49 us (11%)
  local copies, waits for them, and re-layouts  32.6 us (7%)
  between operations  14.8 us (3%)
  starting transfers between devices  6.17 us (1%)
    unnamed x7, waiting for transfers between devices  147 us
    all_gather x1, waiting for transfers between devices, per_device(): lax.all_gather(down_weight, 'row', axis=0, tiled=True)  46.9 us
    all_gather x1, waiting for transfers between devices, per_device(): lax.all_gather(up_weight, 'row', axis=0, tiled=True)  32 us
    scatter-add x8, other arithmetic, up_transpose(): summed = summed.at[:, row_ids[:, slot_index], :].add(product)  21 us
    scatter-add x8, other arithmetic, down_apply(): out_part = out_part.at[:, col_ids[:, slot_index], :].add(product)  21 us
    dot_general x8, matrix products, up_transpose(): jnp.einsum('tjb,jab->tja', grad_piece, panel_blocks[:, slot_index], prefe...  20.1 us
    all_to_all x1, waiting for transfers between devices, per_device(): lax.all_to_all(jnp.stack([tokens] * lax.axis_size('col')), 'col', 0, 0)  18.8 us
    dot_general x8, matrix products, down_apply(): jnp.einsum('tia,iab->tib', hidden_piece, weight_slot, preferred_element_t...  18.4 us
  transfers between devices with their start and end apart: 7, of which 5 were waited for; matrix products, arithmetic and copies ran while one was open for 25% of the time, Pallas kernels for 0%

profile of v1, /device:TPU:1, one launch (start us, length us, event | category | flops | bytes accessed | tf_op | source)
XLA Modules:
  0.0 437.6 jit_solution(13048675917672454199)
XLA Ops:
  7.2 1.7 copy.117
  12.6 6.0 %all-to-all-start = ((bf16[8,128,512]{1,2,0:T(8,128)(2,1)}), bf16[8,128,512]{1,2,0:T(8,128)(2,1)S(1)}, u32[]{:S(2)}, u32[]{:S(2)}) async-start(bf16[8,128,512]{1,2,0:T(8,128)(2,1)} %stack.83), calls=%async_computation | async-start | bytes 2097152 | tf_op jit(solution)/shard_map/all_to_all | solution.py:60
  18.7 18.8 %all-to-all-done = bf16[8,128,512]{1,2,0:T(8,128)(2,1)S(1)} async-done(((bf16[8,128,512]{1,2,0:T(8,128)(2,1)}), bf16[8,128,512]{1,2,0:T(8,128)(2,1)S(1)}, u32[]{:S(2)}, u32[]{:S(2)}) %all-to-all-start) | async-done | bytes 1048608 | tf_op jit(solution)/shard_map/all_to_all | solution.py:60
  61.0 32.0 %all-gather.4.cloned.1.call-done = bf16[16,8,128,128]{3,2,0,1:T(8,128)(2,1)} async-done(((bf16[1,8,128,128]{3,2,0,1:T(8,128)(2,1)}), bf16[16,8,128,128]{3,2,0,1:T(8,128)(2,1)}) %all-gather.4.cloned.1.call-update) | async-done | bytes 4194320 | tf_op jit(solution)/shard_map/all_gather | solution.py:68
  99.6 46.9 %all-gather.6.cloned.1.call-done = bf16[16,8,128,128]{3,2,0,1:T(8,128)(2,1)} async-done(((bf16[1,8,128,128]{3,2,0,1:T(8,128)(2,1)}), bf16[16,8,128,128]{3,2,0,1:T(8,128)(2,1)}) %all-gather.6.cloned.1.call-update) | async-done | bytes 4194320 | tf_op jit(solution)/shard_map/all_gather | solution.py:75
  146.5 2.3 fusion.83
  149.0 2.6 scatter_fusion
  151.6 2.3 fusion.84
  153.9 2.6 scatter_fusion.1
  156.5 2.3 fusion.85
  158.8 2.6 scatter_fusion.2
  161.4 2.3 fusion.86
  163.7 2.6 scatter_fusion.3
  166.3 2.3 fusion.87
  168.6 2.6 scatter_fusion.4
  171.2 2.3 fusion.88
  173.5 2.6 scatter_fusion.5
  176.2 2.3 fusion.89
  178.4 2.8 scatter_fusion.6
  181.2 2.3 fusion.90
  183.5 2.6 scatter_fusion.7
  187.4 1.7 fusion.56
  189.1 1.8 convolution_add_fusion.6
  194.7 2.5 fusion.75
  197.4 2.6 scatter_fusion.8
  200.0 2.5 fusion.76
  202.5 2.6 scatter_fusion.9
  205.1 2.5 fusion.77
  207.6 2.6 scatter_fusion.10
  210.3 2.5 fusion.78
  212.8 2.6 scatter_fusion.11
  215.4 2.5 fusion.79
  217.9 2.6 scatter_fusion.12
  220.5 2.5 fusion.80
  223.0 2.6 scatter_fusion.13
  225.6 2.5 fusion.81
  228.1 2.6 scatter_fusion.14
  230.8 2.5 fusion.82
  233.3 2.8 scatter_fusion.15
  237.2 2.4 fusion.3
  239.7 2.3 fusion.19
  242.0 2.3 fusion.5
  250.5 2.3 fusion.17
  252.9 2.3 fusion.21
  265.4 13.8 %reduce-scatter.11.cloned.1.call-done = bf16[128,4,128]{2,0,1:T(8,128)(2,1)} async-done(((bf16[128,32,128]{2,0,1:T(8,128)(2,1)}), bf16[128,4,128]{2,0,1:T(8,128)(2,1)}) %reduce-scatter.11.cloned.1.call-update) | async-done | bytes 131088 | tf_op jit(solution)/shard_map/reduce_scatter | solution.py:91
  281.1 145.2 %all-reduce.5.cloned.1.call-done = (bf16[16,8,128,128]{3,2,0,1:T(8,128)(2,1)}, bf16[16,8,128,128]{3,2,0,1:T(8,128)(2,1)}) async-done(((bf16[16,8,128,128]{3,2,0,1:T(8,128)(2,1)}, bf16[16,8,128,128]{3,2,0,1:T(8,128)(2,1)}), (bf16[16,8,128,128]{3,2,0,1:T(8,128)(2,1)}, bf16[16,8,128,128]{3,2,0,1:T(8,128)(2,1)})) %all-reduce.5.cloned.1.call-update) | async-done | bytes 8388624
  426.2 2.3 fusion.91
  428.5 2.3 fusion.92
  (144 shorter events, 58.3 us)
Async XLA Ops:
  7.2 11.4 %copy-start.29 = (s32[16,8]{0,1:T(8,128)S(1)}, s32[16,8]{0,1:T(8,128)}, u32[]{:S(2)}) copy-start(s32[16,8]{0,1:T(8,128)} %param.10) | copy-start | bytes 1540
  7.2 11.4 %copy-start.28 = (s32[16,8]{0,1:T(8,128)S(1)}, s32[16,8]{0,1:T(8,128)}, u32[]{:S(2)}) copy-start(s32[16,8]{0,1:T(8,128)} %param.12) | copy-start | bytes 1540
  7.2 41.7 %all-gather.8.cloned.1.call-start = ((), (), s32[]{:S(2)}) async-start(), calls=%async_computation.6 | async-start | bytes 1179648 | tf_op jit(solution)/shard_map/all_gather | solution.py:62
  8.9 84.1 %all-gather.4.cloned.1.call-start = ((), (), s32[]{:S(2)}) async-start(), calls=%async_computation.3 | async-start | bytes 4456448 | tf_op jit(solution)/shard_map/all_gather | solution.py:68
  9.7 136.8 %all-gather.6.cloned.1.call-start = ((), (), s32[]{:S(2)}) async-start(), calls=%async_computation.4 | async-start | bytes 4456448 | tf_op jit(solution)/shard_map/all_gather | solution.py:75
  12.6 25.0 %all-to-all-start = ((bf16[8,128,512]{1,2,0:T(8,128)(2,1)}), bf16[8,128,512]{1,2,0:T(8,128)(2,1)S(1)}, u32[]{:S(2)}, u32[]{:S(2)}) async-start(bf16[8,128,512]{1,2,0:T(8,128)(2,1)} %stack.83), calls=%async_computation | async-start | bytes 2097152 | tf_op jit(solution)/shard_map/all_to_all | solution.py:60
  18.5 245.1 %reduce-scatter.9.cloned.1.call-start = ((), (), s32[]{:S(2)}) async-start(), calls=%async_computation.5 | async-start | bytes 1179648 | tf_op jit(solution)/shard_map/reduce_scatter | solution.py:80
  38.9 54.1 %copy-start.2 = (bf16[16,128,128]{2,1,0:T(8,128)(2,1)}, bf16[16,128,128]{2,1,0:T(8,128)(2,1)S(1)}, u32[]{:S(2)}) copy-start(bf16[16,128,128]{2,1,0:T(8,128)(2,1)S(1)} %gather_fusion) | copy-start | bytes 1572868
  51.1 136.2 %copy-start.3 = (bf16[16,128,128]{2,1,0:T(8,128)(2,1)}, bf16[16,128,128]{2,1,0:T(8,128)(2,1)S(1)}, u32[]{:S(2)}) copy-start(bf16[16,128,128]{2,1,0:T(8,128)(2,1)S(1)} %gather_fusion.8) | copy-start | bytes 1572868
  52.6 42.0 %copy-start.24 = (bf16[16,128,128]{2,1,0:T(8,128)(2,1)S(1)}, bf16[16,128,128]{2,1,0:T(8,128)(2,1)}, u32[]{:S(2)}) copy-start(bf16[16,128,128]{2,1,0:T(8,128)(2,1)} %gather_fusion.1) | copy-start | bytes 1572868
  56.8 39.3 %copy-start.22 = (bf16[16,128,128]{2,1,0:T(8,128)(2,1)S(1)}, bf16[16,128,128]{2,1,0:T(8,128)(2,1)}, u32[]{:S(2)}) copy-start(bf16[16,128,128]{2,1,0:T(8,128)(2,1)} %gather_fusion.2) | copy-start | bytes 1572868
  93.0 3.1 copy-start
  93.0 3.4 copy-start.20
  94.6 2.2 copy-start.18
  96.1 1.1 copy-start.16
  96.5 1.1 copy-start.14
  96.8 1.1 copy-start.27
  187.3 3.6 copy-start.12
  187.3 92.0 %reduce-scatter.11.cloned.1.call-start = ((), (), s32[]{:S(2)}) async-start(), calls=%async_computation.7 | async-start | bytes 1179648 | tf_op jit(solution)/shard_map/reduce_scatter | solution.py:91
  187.3 3.5 copy-start.1
  187.4 4.1 copy-start.10
  189.1 2.9 copy-start.8
  190.9 1.7 copy-start.6
  191.5 1.6 copy-start.4
  192.0 1.6 copy-start.25
  192.0 1.6 copy-start.31
  237.2 8.3 %copy-start.21 = (bf16[16,128,128]{2,1,0:T(8,128)(2,1)S(1)}, bf16[16,128,128]{2,1,0:T(8,128)(2,1)}, u32[]{:S(2)}) copy-start(bf16[16,128,128]{2,1,0:T(8,128)(2,1)} %gather_fusion.3) | copy-start | bytes 1572868
  237.2 7.1 %copy-start.23 = (bf16[16,128,128]{2,1,0:T(8,128)(2,1)S(1)}, bf16[16,128,128]{2,1,0:T(8,128)(2,1)}, u32[]{:S(2)}) copy-start(bf16[16,128,128]{2,1,0:T(8,128)(2,1)} %gather_fusion.2) | copy-start | bytes 1572868
  237.2 9.5 %copy-start.19 = (bf16[16,128,128]{2,1,0:T(8,128)(2,1)S(1)}, bf16[16,128,128]{2,1,0:T(8,128)(2,1)}, u32[]{:S(2)}) copy-start(bf16[16,128,128]{2,1,0:T(8,128)(2,1)} %gather_fusion.4) | copy-start | bytes 1572868
  239.7 8.3 %copy-start.17 = (bf16[16,128,128]{2,1,0:T(8,128)(2,1)S(1)}, bf16[16,128,128]{2,1,0:T(8,128)(2,1)}, u32[]{:S(2)}) copy-start(bf16[16,128,128]{2,1,0:T(8,128)(2,1)} %gather_fusion.5) | copy-start | bytes 1572868
  242.0 7.3 %copy-start.15 = (bf16[16,128,128]{2,1,0:T(8,128)(2,1)S(1)}, bf16[16,128,128]{2,1,0:T(8,128)(2,1)}, u32[]{:S(2)}) copy-start(bf16[16,128,128]{2,1,0:T(8,128)(2,1)} %gather_fusion.6) | copy-start | bytes 1572868
  246.8 8.4 %copy-start.13 = (bf16[16,128,128]{2,1,0:T(8,128)(2,1)S(1)}, bf16[16,128,128]{2,1,0:T(8,128)(2,1)}, u32[]{:S(2)}) copy-start(bf16[16,128,128]{2,1,0:T(8,128)(2,1)} %gather_fusion.10) | copy-start | bytes 1572868
  248.0 8.4 %copy-start.11 = (bf16[16,128,128]{2,1,0:T(8,128)(2,1)S(1)}, bf16[16,128,128]{2,1,0:T(8,128)(2,1)}, u32[]{:S(2)}) copy-start(bf16[16,128,128]{2,1,0:T(8,128)(2,1)} %gather_fusion.11) | copy-start | bytes 1572868
  249.2 8.3 %copy-start.9 = (bf16[16,128,128]{2,1,0:T(8,128)(2,1)S(1)}, bf16[16,128,128]{2,1,0:T(8,128)(2,1)}, u32[]{:S(2)}) copy-start(bf16[16,128,128]{2,1,0:T(8,128)(2,1)} %gather_fusion.12) | copy-start | bytes 1572868
  250.5 8.3 %copy-start.7 = (bf16[16,128,128]{2,1,0:T(8,128)(2,1)S(1)}, bf16[16,128,128]{2,1,0:T(8,128)(2,1)}, u32[]{:S(2)}) copy-start(bf16[16,128,128]{2,1,0:T(8,128)(2,1)} %gather_fusion.13) | copy-start | bytes 1572868
  250.5 175.7 %all-reduce.5.cloned.1.call-start = ((), (), s32[]{:S(2)}) async-start(), calls=%async_computation.8 | async-start | bytes 16777216
  252.9 7.1 %copy-start.5 = (bf16[16,128,128]{2,1,0:T(8,128)(2,1)S(1)}, bf16[16,128,128]{2,1,0:T(8,128)(2,1)}, u32[]{:S(2)}) copy-start(bf16[16,128,128]{2,1,0:T(8,128)(2,1)} %gather_fusion.14) | copy-start | bytes 1572868
  255.2 6.0 %copy-start.26 = (bf16[16,128,128]{2,1,0:T(8,128)(2,1)S(1)}, bf16[16,128,128]{2,1,0:T(8,128)(2,1)}, u32[]{:S(2)}) copy-start(bf16[16,128,128]{2,1,0:T(8,128)(2,1)} %gather_fusion.15) | copy-start | bytes 1572868
  262.4 0.7 copy-start.30
Sparse Core Ops, SparseCore 0:
  10.3 29.0 all-gather.7
  41.6 51.3 all-gather.3
  95.2 51.2 all-gather.5
  187.4 28.6 reduce-scatter.8
  250.6 28.6 reduce-scatter.10
  282.9 143.2 all-reduce.4
